TPU v7x, 128 devices: a whole 4x4x4 slice. The times are simulated.
128 devices in a mesh: row: 8 (over y, core), col: 16 (over z, x).
Axes of the slice: x: 4, y: 4, z: 4, core: 2. Of those that a mesh axis runs over, the one named last changes fastest.
Arguments:
- amplitudes: bfloat16 [16, 16, 4, 128, 128], P('row', 'col'), may hold values from -6 to 6
- cholesky: bfloat16 [16, 16, 10, 128, 128], P('row', 'col'), may hold values from -0.5 to 0.5, as said below
- tile_mask: int32 [16, 16], P('row', 'col'), may hold values 0 or 1
Outputs:
- antisymmetrized: bfloat16 [16, 16, 4, 128, 128], P('row', 'col')
Inputs may be any that keep to these rules, and one draw needn't show every extreme that they name: cholesky is symmetric: cholesky[a,c,q,x,u] equals cholesky[c,a,q,u,x].
All inputs are finite; a program needn't handle non-finite values. No bound on the sum of `tile_mask` on one device may be relied on, other than what follows from the above.
Results may differ from a plain program's by a relative error of at most 0.0059.
Values may be sent and summed in bfloat16 or wider, within the bound.
A program may use at most 128 MiB of HBM per device.

v0:
```python
import math
import jax
import jax.numpy as jnp
from jax import lax
from jax.sharding import PartitionSpec as P


def from_partner(value, axis, apart):
    mask = 2**apart
    pairs = [(source, source ^ mask) for source in range(lax.axis_size(axis))]
    return lax.ppermute(value, axis, pairs)


def flip_row(tile_set, bit_pos):
    bit_value = lax.axis_index("row") >> bit_pos & 1
    kept = lax.dynamic_index_in_dim(tile_set, bit_value, 0, keepdims=False)
    outgoing = lax.dynamic_index_in_dim(tile_set, 1 - bit_value, 0, keepdims=False)
    incoming = from_partner(outgoing, "row", bit_pos)
    slot_zero = jnp.where(bit_value == 0, kept, incoming)
    slot_one = jnp.where(bit_value == 0, incoming, kept)
    return jnp.stack([slot_zero, slot_one])


def flip_col(tile_set, bit_pos):
    bit_value = lax.axis_index("col") >> bit_pos & 1
    kept = lax.dynamic_index_in_dim(tile_set, bit_value, 0, keepdims=False)
    outgoing = lax.dynamic_index_in_dim(tile_set, 1 - bit_value, 0, keepdims=False)
    incoming = from_partner(outgoing, "col", bit_pos)
    slot_zero = jnp.where(bit_value == 0, kept, incoming)
    slot_one = jnp.where(bit_value == 0, incoming, kept)
    return jnp.stack([slot_zero, slot_one])


def mirror_cascade(tile_set):
    col_bits = lax.axis_size("col").bit_length() - 1
    tile_set = flip_col(tile_set, 0)
    for bit_pos in range(1, col_bits):
        tile_set = flip_row(tile_set, bit_pos - 1)
        tile_set = flip_col(tile_set, bit_pos)
        tile_set = flip_row(tile_set, bit_pos - 1)
    return tile_set


def body(amplitudes, cholesky, tile_mask):
    tile_rows = amplitudes.shape[0]
    pair_count = amplitudes.shape[2]
    tile_edge = amplitudes.shape[3]
    vectors = cholesky.shape[2]
    occupied = math.isqrt(pair_count)
    column = lax.all_gather(cholesky, "row", axis=0, tiled=True)
    column_mats = jnp.transpose(column[:, 0], (0, 2, 1, 3)).reshape(
        column.shape[0], tile_edge, vectors * tile_edge
    )
    amp_block = lax.all_gather(amplitudes, "col", axis=1, tiled=True)
    mask_block = lax.all_gather(tile_mask, "col", axis=1, tiled=True)
    tile_count = amp_block.shape[1]
    masked = amp_block * mask_block.astype(jnp.bfloat16)[:, :, None, None, None]
    masked = masked.reshape(amp_block.shape[0], tile_count, pair_count * tile_edge, tile_edge)
    halves = jnp.einsum("cnmv,nvz->cmz", masked, column_mats, preferred_element_type=jnp.float32)
    halves = halves.astype(jnp.bfloat16).reshape(
        tile_rows, pair_count, tile_edge, vectors, tile_edge
    )
    spread = lax.all_gather(cholesky, "col", axis=1, tiled=True)
    ladder = lax.psum_scatter(
        jnp.einsum("caqux,cpuqy->apxy", spread, halves, preferred_element_type=jnp.float32),
        "row",
        scatter_dimension=0,
        tiled=True,
    )
    rounded = ladder.astype(jnp.bfloat16)
    mirror = mirror_cascade(rounded)
    own_tiles = lax.optimization_barrier(rounded).astype(jnp.float32)
    flipped = mirror.reshape(tile_rows, occupied, occupied, tile_edge, tile_edge)
    flipped = jnp.transpose(flipped, (0, 2, 1, 4, 3)).reshape(
        tile_rows, pair_count, tile_edge, tile_edge
    )
    result_tiles = (own_tiles - flipped.astype(jnp.float32)).astype(jnp.bfloat16)
    return result_tiles.reshape(tile_rows, 1, pair_count, tile_edge, tile_edge)


def solution(mesh):
    in_specs = (
        P("row", "col", None, None, None),
        P("row", "col", None, None, None),
        P("row", "col"),
    )
    out_specs = P("row", "col", None, None, None)
    return jax.shard_map(body, mesh=mesh, in_specs=in_specs, out_specs=out_specs, check_vma=False)
```

profile of v0, /device:TPU:0, one launch (start us, length us, event | category | flops | bytes accessed | tf_op | source)
XLA Modules:
  0.0 314.2 jit_solution(16139904179975113621)
XLA Ops:
  8.7 22.0 %all-gather = s32[16,1,2]{2,1,0:T(1,128)S(1)} all-gather(s32[1,1,2]{2,1,0:T(1,128)} %bitcast.173), channel_id=1, replica_groups=mesh['row'=8,'col'=16] {'col'}, dimensions={0}, use_global_device_ids=true | all-gather | bytes 136 | tf_op jit(solution)/shard_map/all_gather | solution.py:55
  32.7 31.0 %all-gather.5.cloned.1.call-done = bf16[2,16,4,128,128]{4,3,2,1,0:T(8,128)(2,1)} async-done(((bf16[2,1,4,128,128]{4,3,2,1,0:T(8,128)(2,1)}), bf16[2,16,4,128,128]{4,3,2,1,0:T(8,128)(2,1)}) %all-gather.5.cloned.1.call-update) | async-done | bytes 4194320 | tf_op jit(solution)/shard_map/all_gather | solution.py:54
  63.7 4.6 %broadcast_multiply_fusion = bf16[2,16,4,128,128]{4,3,2,1,0:T(8,128)(2,1)} fusion(bf16[2,16,4,128,128]{4,3,2,1,0:T(8,128)(2,1)} %all-gather.5.cloned.1.call-done, bf16[2,16]{1,0:T(2,128)(2,1)S(1)} %convert_bitcast_fusion.1), kind=kLoop, calls=%fused_computation.5 | loop fusion | flops 2097152 | bytes 8388672 | tf_op jit(solution)/shard_map/mul | solution.py:57
  68.3 33.3 %all-gather.7.cloned.1.call-done = bf16[16,1,10,128,128]{4,3,2,1,0:T(8,128)(2,1)} async-done(((bf16[2,1,10,128,128]{4,3,2,1,0:T(8,128)(2,1)}), bf16[16,1,10,128,128]{4,3,2,1,0:T(8,128)(2,1)}) %all-gather.7.cloned.1.call-update) | async-done | bytes 5242896 | tf_op jit(solution)/shard_map/all_gather | solution.py:50
  101.6 7.8 %copy.36 = bf16[16,1,10,128,128]{3,4,2,0,1:T(8,128)(2,1)} copy(bf16[16,1,10,128,128]{4,3,2,1,0:T(8,128)(2,1)} %all-gather.7.cloned.1.call-done) | data formatting | bytes 10485760 | tf_op jit(solution)/shard_map/all_gather | solution.py:50
  109.4 9.0 %bitcast_convert_fusion = bf16[2,512,1280]{2,1,0:T(8,128)(2,1)S(1)} fusion(bf16[2,16,512,128]{3,2,1,0:T(8,128)(2,1)} %bitcast.167, bf16[16,128,1280,1]{1,2,0,3:T(8,128)(2,1)} %bitcast.166), kind=kOutput, calls=%fused_computation.2 | convolution fusion | flops 5370019840 | bytes 12058624 | tf_op jit(solution)/shard_map/cnmv,nvz->cmz/dot_general | solution.py:59
  118.3 3.2 %reshape.36 = bf16[2,4,128,10,128]{4,3,2,1,0:T(8,128)(2,1)} reshape(bf16[2,512,1280]{2,1,0:T(8,128)(2,1)S(1)} %bitcast_convert_fusion) | data formatting | bytes 5242880 | tf_op jit(solution)/shard_map/reshape | solution.py:60
  121.5 62.8 %all-gather.9.cloned.1.call-done = bf16[2,16,10,128,128]{4,3,2,0,1:T(8,128)(2,1)} async-done(((bf16[2,1,10,128,128]{4,3,2,0,1:T(8,128)(2,1)}), bf16[2,16,10,128,128]{4,3,2,0,1:T(8,128)(2,1)}) %all-gather.9.cloned.1.call-update) | async-done | bytes 10485776 | tf_op jit(solution)/shard_map/all_gather | solution.py:63
  184.3 10.9 %fusion.3 = f32[16,4,128,128]{2,3,0,1:T(8,128)} fusion(bf16[2,16,10,128,128]{4,3,2,0,1:T(8,128)(2,1)} %all-gather.9.cloned.1.call-done, bf16[2,4,128,10,128,1]{4,3,2,1,0,5:T(8,128)(2,1)} %bitcast.168), kind=kOutput, calls=%fused_computation.4 | convolution fusion | flops 5368709120 | bytes 17301504 | tf_op jit(solution)/shard_map/caqux,cpuqy->apxy/dot_general | solution.py:65
  195.2 58.5 %all-reduce.2 = bf16[16,4,128,128]{2,3,0,1:T(8,128)(2,1)S(1)} all-reduce(f32[16,4,128,128]{2,3,0,1:T(8,128)} %fusion.3), channel_id=2, replica_groups=mesh['row'=8,'col'=16] {'row'}, use_global_device_ids=true, to_apply=%region_0.0.clone | all-reduce | flops 1048576 | bytes 6291456
  253.9 1.5 collective-permute-start
  255.4 3.5 %collective-permute-done = bf16[4,128,128]{2,1,0:T(8,128)(2,1)S(1)} collective-permute-done((bf16[4,128,128]{2,1,0:T(8,128)(2,1)S(1)}, bf16[4,128,128]{2,1,0:T(8,128)(2,1)S(1)}, u32[]{:S(2)}, u32[]{:S(2)}) %collective-permute-start) | collective-permute-done | bytes 131104 | tf_op jit(solution)/shard_map/ppermute | solution.py:11
  259.2 1.3 collective-permute-done.1
  260.6 3.0 collective-permute-start.2
  263.7 4.1 %collective-permute-done.2 = bf16[4,128,128]{2,1,0:T(8,128)(2,1)S(1)} collective-permute-done((bf16[4,128,128]{2,1,0:T(8,128)(2,1)S(1)}, bf16[4,128,128]{2,1,0:T(8,128)(2,1)S(1)}, u32[]{:S(2)}, u32[]{:S(2)}) %collective-permute-start.2) | collective-permute-done | bytes 131104 | tf_op jit(solution)/shard_map/ppermute | solution.py:11
  268.0 1.3 collective-permute-done.3
  269.6 5.5 %collective-permute-done.4 = bf16[4,128,128]{2,1,0:T(8,128)(2,1)S(1)} collective-permute-done((bf16[4,128,128]{2,1,0:T(8,128)(2,1)S(1)}, bf16[4,128,128]{2,1,0:T(8,128)(2,1)S(1)}, u32[]{:S(2)}, u32[]{:S(2)}) %collective-permute-start.4) | collective-permute-done | bytes 131104 | tf_op jit(solution)/shard_map/ppermute | solution.py:11
  275.3 1.4 collective-permute-start.5
  276.6 3.7 %collective-permute-done.5 = bf16[4,128,128]{2,1,0:T(8,128)(2,1)S(1)} collective-permute-done((bf16[4,128,128]{2,1,0:T(8,128)(2,1)S(1)}, bf16[4,128,128]{2,1,0:T(8,128)(2,1)S(1)}, u32[]{:S(2)}, u32[]{:S(2)}) %collective-permute-start.5) | collective-permute-done | bytes 131104 | tf_op jit(solution)/shard_map/ppermute | solution.py:11
  280.9 5.7 %collective-permute-done.6 = bf16[4,128,128]{2,1,0:T(8,128)(2,1)S(1)} collective-permute-done((bf16[4,128,128]{2,1,0:T(8,128)(2,1)S(1)}, bf16[4,128,128]{2,1,0:T(8,128)(2,1)S(1)}, u32[]{:S(2)}, u32[]{:S(2)}) %collective-permute-start.6) | collective-permute-done | bytes 131104 | tf_op jit(solution)/shard_map/ppermute | solution.py:11
  286.8 6.4 %collective-permute-done.7 = bf16[4,128,128]{2,1,0:T(8,128)(2,1)S(1)} collective-permute-done((bf16[4,128,128]{2,1,0:T(8,128)(2,1)S(1)}, bf16[4,128,128]{2,1,0:T(8,128)(2,1)S(1)}, u32[]{:S(2)}, u32[]{:S(2)}) %collective-permute-start.7) | collective-permute-done | bytes 131104 | tf_op jit(solution)/shard_map/ppermute | solution.py:11
  293.4 3.0 collective-permute-start.8
  296.4 3.6 %collective-permute-done.8 = bf16[4,128,128]{2,1,0:T(8,128)(2,1)S(1)} collective-permute-done((bf16[4,128,128]{2,1,0:T(8,128)(2,1)S(1)}, bf16[4,128,128]{2,1,0:T(8,128)(2,1)S(1)}, u32[]{:S(2)}, u32[]{:S(2)}) %collective-permute-start.8) | collective-permute-done | bytes 131104 | tf_op jit(solution)/shard_map/ppermute | solution.py:11
  300.2 6.5 %collective-permute-done.9 = bf16[4,128,128]{2,1,0:T(8,128)(2,1)S(1)} collective-permute-done((bf16[4,128,128]{2,1,0:T(8,128)(2,1)S(1)}, bf16[4,128,128]{2,1,0:T(8,128)(2,1)S(1)}, u32[]{:S(2)}, u32[]{:S(2)}) %collective-permute-start.9) | collective-permute-done | bytes 131104 | tf_op jit(solution)/shard_map/ppermute | solution.py:11
  (40 shorter events, 6.8 us)
Async XLA Ops:
  6.5 57.2 %all-gather.5.cloned.1.call-start = ((), (), s32[]{:S(2)}) async-start(), calls=%async_computation | async-start | bytes 4456448 | tf_op jit(solution)/shard_map/all_gather | solution.py:54
  7.3 94.3 %all-gather.7.cloned.1.call-start = ((), (), s32[]{:S(2)}) async-start(), calls=%async_computation.1 | async-start | bytes 5898240 | tf_op jit(solution)/shard_map/all_gather | solution.py:50
  8.0 176.3 %all-gather.9.cloned.1.call-start = ((), (), s32[]{:S(2)}) async-start(), calls=%async_computation.2 | async-start | bytes 11141120 | tf_op jit(solution)/shard_map/all_gather | solution.py:63
  253.9 5.0 %collective-permute-start = (bf16[4,128,128]{2,1,0:T(8,128)(2,1)S(1)}, bf16[4,128,128]{2,1,0:T(8,128)(2,1)S(1)}, u32[]{:S(2)}, u32[]{:S(2)}) collective-permute-start(bf16[4,128,128]{2,1,0:T(8,128)(2,1)S(1)} %dynamic-slice_bitcast_fusion), channel_id=1, source_target_pairs={{0,1},{1,0},{2,3},{3,2},{4,5},{5,4},{6,7},{7,6},{8,9},{9,8},{10,11... | collective-permute-start | bytes 393224 | tf_op jit(solution)/shard_map/ppermute | solution.py:11
  259.1 1.4 collective-permute-start.1
  260.6 7.1 %collective-permute-start.2 = (bf16[4,128,128]{2,1,0:T(8,128)(2,1)S(1)}, bf16[4,128,128]{2,1,0:T(8,128)(2,1)S(1)}, u32[]{:S(2)}, u32[]{:S(2)}) collective-permute-start(bf16[4,128,128]{2,1,0:T(8,128)(2,1)S(1)} %fusion.38), channel_id=1, source_target_pairs={{0,2},{1,3},{2,0},{3,1},{4,6},{5,7},{6,4},{7,5},{8,10},{9,11},{10,... | collective-permute-start | bytes 393224 | tf_op jit(solution)/shard_map/ppermute | solution.py:11
  267.9 1.4 collective-permute-start.3
  269.5 5.6 %collective-permute-start.4 = (bf16[4,128,128]{2,1,0:T(8,128)(2,1)S(1)}, bf16[4,128,128]{2,1,0:T(8,128)(2,1)S(1)}, u32[]{:S(2)}, u32[]{:S(2)}) collective-permute-start(bf16[4,128,128]{2,1,0:T(8,128)(2,1)S(1)} %fusion.30), channel_id=1, source_target_pairs={{0,32},{16,48},{32,0},{48,16},{64,96},{80,112},{96,64},{112,80},{1... | collective-permute-start | bytes 393224 | tf_op jit(solution)/shard_map/ppermute | solution.py:11
  275.3 5.0 %collective-permute-start.5 = (bf16[4,128,128]{2,1,0:T(8,128)(2,1)S(1)}, bf16[4,128,128]{2,1,0:T(8,128)(2,1)S(1)}, u32[]{:S(2)}, u32[]{:S(2)}) collective-permute-start(bf16[4,128,128]{2,1,0:T(8,128)(2,1)S(1)} %fusion.26), channel_id=1, source_target_pairs={{0,4},{1,5},{2,6},{3,7},{4,0},{5,1},{6,2},{7,3},{8,12},{9,13},{10,... | collective-permute-start | bytes 393224 | tf_op jit(solution)/shard_map/ppermute | solution.py:11
  280.4 6.1 %collective-permute-start.6 = (bf16[4,128,128]{2,1,0:T(8,128)(2,1)S(1)}, bf16[4,128,128]{2,1,0:T(8,128)(2,1)S(1)}, u32[]{:S(2)}, u32[]{:S(2)}) collective-permute-start(bf16[4,128,128]{2,1,0:T(8,128)(2,1)S(1)} %fusion.22), channel_id=1, source_target_pairs={{0,32},{16,48},{32,0},{48,16},{64,96},{80,112},{96,64},{112,80},{1... | collective-permute-start | bytes 393224 | tf_op jit(solution)/shard_map/ppermute | solution.py:11
  286.7 6.6 %collective-permute-start.7 = (bf16[4,128,128]{2,1,0:T(8,128)(2,1)S(1)}, bf16[4,128,128]{2,1,0:T(8,128)(2,1)S(1)}, u32[]{:S(2)}, u32[]{:S(2)}) collective-permute-start(bf16[4,128,128]{2,1,0:T(8,128)(2,1)S(1)} %fusion.18), channel_id=1, source_target_pairs={{0,64},{16,80},{32,96},{48,112},{64,0},{80,16},{96,32},{112,48},{1... | collective-permute-start | bytes 393224 | tf_op jit(solution)/shard_map/ppermute | solution.py:11
  293.4 6.6 %collective-permute-start.8 = (bf16[4,128,128]{2,1,0:T(8,128)(2,1)S(1)}, bf16[4,128,128]{2,1,0:T(8,128)(2,1)S(1)}, u32[]{:S(2)}, u32[]{:S(2)}) collective-permute-start(bf16[4,128,128]{2,1,0:T(8,128)(2,1)S(1)} %fusion.14), channel_id=1, source_target_pairs={{0,8},{1,9},{2,10},{3,11},{4,12},{5,13},{6,14},{7,15},{8,0},{9,1},... | collective-permute-start | bytes 393224 | tf_op jit(solution)/shard_map/ppermute | solution.py:11
  300.1 6.6 %collective-permute-start.9 = (bf16[4,128,128]{2,1,0:T(8,128)(2,1)S(1)}, bf16[4,128,128]{2,1,0:T(8,128)(2,1)S(1)}, u32[]{:S(2)}, u32[]{:S(2)}) collective-permute-start(bf16[4,128,128]{2,1,0:T(8,128)(2,1)S(1)} %fusion.10), channel_id=1, source_target_pairs={{0,64},{16,80},{32,96},{48,112},{64,0},{80,16},{96,32},{112,48},{1... | collective-permute-start | bytes 393224 | tf_op jit(solution)/shard_map/ppermute | solution.py:11
Sparse Core Ops, SparseCore 0:
  9.5 54.1 all-gather.4
  65.4 36.0 all-gather.6
  103.7 80.5 all-gather.8
where the time goes:
time: 315 us; the launch traced here: 314 us
  waiting for transfers between devices  171 us (54%)
  blocking collectives  80.5 us (26%)
  matrix products  19.9 us (6%)
  between operations  14 us (4%)
  local copies, waits for them, and re-layouts  12.7 us (4%)
  starting transfers between devices  9.81 us (3%)
  other arithmetic  6.55 us (2%)
    all_gather x1, waiting for transfers between devices, body(): spread = lax.all_gather(cholesky, 'col', axis=1, tiled=True)  62.8 us
    unnamed x1, blocking collectives  58.5 us
    ppermute x10, waiting for transfers between devices, from_partner(): return lax.ppermute(value, axis, pairs)  41.7 us
    all_gather x1, waiting for transfers between devices, body(): column = lax.all_gather(cholesky, 'row', axis=0, tiled=True)  33.3 us
    all_gather x1, waiting for transfers between devices, body(): amp_block = lax.all_gather(amplitudes, 'col', axis=1, tiled=True)  31 us
    all_gather x1, blocking collectives, body(): mask_block = lax.all_gather(tile_mask, 'col', axis=1, tiled=True)  22 us
    dot_general x1, matrix products, body(): jnp.einsum('caqux,cpuqy->apxy', spread, halves, preferred_element_type=jn...  10.9 us
    ppermute x10, starting transfers between devices, from_partner(): return lax.ppermute(value, axis, pairs)  9.73 us
  transfers between devices with their start and end apart: 13, of which 13 were waited for; matrix products, arithmetic and copies ran while one was open for 8% of the time, Pallas kernels for 0%

commit v1 on v0

--- a/solution.py
+++ b/solution.py
@@ -51,7 +51,10 @@
     column_mats = jnp.transpose(column[:, 0], (0, 2, 1, 3)).reshape(
         column.shape[0], tile_edge, vectors * tile_edge
     )
-    amp_block = lax.all_gather(amplitudes, "col", axis=1, tiled=True)
+    _change_figure = lambda u_in, link_axis: jnp.concatenate(
+        lax.all_to_all(jnp.stack(lax.axis_size(link_axis) * [u_in], 0), link_axis, 0, 0), 1
+    )
+    amp_block = _change_figure(amplitudes, link_axis="col")
     mask_block = lax.all_gather(tile_mask, "col", axis=1, tiled=True)
     tile_count = amp_block.shape[1]
     masked = amp_block * mask_block.astype(jnp.bfloat16)[:, :, None, None, None]

time: 315 us -> 272 us (0.86)
  waiting for transfers between devices: 171 us -> 55.1 us
  blocking collectives: 80.5 us -> 141 us
  starting transfers between devices: 9.81 us -> 17.8 us
  local copies, waits for them, and re-layouts: 12.7 us -> 16.2 us
    all_gather x1, blocking collectives: 22 us -> 82.6 us  [body(): mask_block = lax.all_gather(tile_mask, 'col', axis=1, tiled=True)]
    all_gather x1, waiting for transfers between devices: 62.8 us -> 11.9 us  [body(): spread = lax.all_gather(cholesky, 'col', axis=1, tiled=True)]
    all_gather x1, waiting for transfers between devices: 33.3 us -> 0.01 us  [body(): column = lax.all_gather(cholesky, 'row', axis=0, tiled=True)]
    all_gather x1 -> x0, waiting for transfers between devices: 31 us -> none  [body(): amp_block = lax.all_gather(amplitudes, 'col', axis=1, tiled=True)]
    all_to_all x0 -> x1, starting transfers between devices: none -> 8.14 us  [body(): lax.all_to_all(jnp.stack(lax.axis_size(link_axis) * [u_in], 0), link_axis...]
    another operation x0 -> x1, local copies, waits for them, and re-layouts: none -> 3.98 us  [body(): jnp.stack(lax.axis_size(link_axis) * [u_in], 0)]
  transfers between devices with their start and end apart: 13 -> 13, of which waited for: 13 -> 11; matrix products, arithmetic and copies ran while one was open for 8% -> 11% of each run, Pallas kernels for 0% -> 0%
where the time goes in v1:
time: 272 us; the launch traced here: 271 us
  blocking collectives  141 us (52%)
  waiting for transfers between devices  55.1 us (20%)
  matrix products  20 us (7%)
  starting transfers between devices  17.8 us (7%)
  local copies, waits for them, and re-layouts  16.2 us (6%)
  between operations  14.3 us (5%)
  other arithmetic  6.55 us (2%)
    all_gather x1, blocking collectives, body(): mask_block = lax.all_gather(tile_mask, 'col', axis=1, tiled=True)  82.6 us
    unnamed x1, blocking collectives  58.5 us
    ppermute x10, waiting for transfers between devices, from_partner(): return lax.ppermute(value, axis, pairs)  41.8 us
    all_gather x1, waiting for transfers between devices, body(): spread = lax.all_gather(cholesky, 'col', axis=1, tiled=True)  11.9 us
    dot_general x1, matrix products, body(): jnp.einsum('caqux,cpuqy->apxy', spread, halves, preferred_element_type=jn...  10.9 us
    ppermute x10, starting transfers between devices, from_partner(): return lax.ppermute(value, axis, pairs)  9.64 us
    dot_general x1, matrix products, body(): jnp.einsum('cnmv,nvz->cmz', masked, column_mats, preferred_element_type=j...  9.16 us
    all_to_all x1, starting transfers between devices, body(): lax.all_to_all(jnp.stack(lax.axis_size(link_axis) * [u_in], 0), link_axis...  8.14 us
  transfers between devices with their start and end apart: 13, of which 11 were waited for; matrix products, arithmetic and copies ran while one was open for 11% of the time, Pallas kernels for 0%

profile of v1, /device:TPU:0, one launch (start us, length us, event | category | flops | bytes accessed | tf_op | source)
XLA Modules:
  0.0 271.1 jit_solution(1501245401231915488)
XLA Ops:
  8.0 4.0 %stack.109 = bf16[16,2,1,4,128,128]{5,4,3,1,2,0:T(8,128)(2,1)} broadcast(bf16[2,4,128,128]{3,2,1,0:T(8,128)(2,1)} %bitcast.177), dimensions={1,3,4,5} | broadcast | bytes 4456448 | tf_op jit(solution)/shard_map/stack | solution.py:55
  12.0 8.1 %all-to-all-start = ((bf16[16,2,1,4,128,128]{5,4,3,1,2,0:T(8,128)(2,1)}), bf16[16,2,1,4,128,128]{5,4,3,1,2,0:T(8,128)(2,1)}, u32[]{:S(2)}, u32[]{:S(2)}) async-start(bf16[16,2,1,4,128,128]{5,4,3,1,2,0:T(8,128)(2,1)} %stack.109), calls=%async_computation | async-start | bytes 8388608 | tf_op jit(solution)/shard_map/all_to_all | solution.py:55
  20.2 82.6 %all-gather = s32[16,1,2]{2,1,0:T(1,128)S(1)} all-gather(s32[1,1,2]{2,1,0:T(1,128)S(1)} %bitcast.178), channel_id=1, replica_groups=mesh['row'=8,'col'=16] {'col'}, dimensions={0}, use_global_device_ids=true | all-gather | bytes 136 | tf_op jit(solution)/shard_map/all_gather | solution.py:58
  104.2 4.5 %bitcast_multiply_fusion = bf16[2,16,1,4,128,128]{5,4,3,0,2,1:T(8,128)(2,1)} fusion(bf16[16,2,1,4,128,128]{5,4,3,1,2,0:T(8,128)(2,1)} %all-to-all-done, bf16[2,16]{0,1:T(8,128)(2,1)S(1)} %copy.39), kind=kLoop, calls=%fused_computation.3 | loop fusion | flops 2097152 | bytes 8388672 | tf_op jit(solution)/shard_map/mul | solution.py:60
  108.8 7.9 %copy.40 = bf16[16,1,10,128,128]{3,4,2,0,1:T(8,128)(2,1)} copy(bf16[16,1,10,128,128]{4,3,2,1,0:T(8,128)(2,1)} %all-gather.4.cloned.1.call-done) | data formatting | bytes 10485760 | tf_op jit(solution)/shard_map/all_gather | solution.py:50
  116.6 9.2 %bitcast_convert_fusion = bf16[2,512,1280]{2,1,0:T(8,128)(2,1)S(1)} fusion(bf16[2,16,512,128]{3,2,0,1:T(8,128)(2,1)} %bitcast.171, bf16[16,128,1280,1]{1,2,3,0:T(8,128)(2,1)} %bitcast.170), kind=kOutput, calls=%fused_computation.2 | convolution fusion | flops 5370019840 | bytes 12058624 | tf_op jit(solution)/shard_map/cnmv,nvz->cmz/dot_general | solution.py:62
  125.8 3.2 %reshape.44 = bf16[2,4,128,10,128]{4,3,2,1,0:T(8,128)(2,1)} reshape(bf16[2,512,1280]{2,1,0:T(8,128)(2,1)S(1)} %bitcast_convert_fusion) | data formatting | bytes 5242880 | tf_op jit(solution)/shard_map/reshape | solution.py:63
  129.0 11.9 %all-gather.6.cloned.1.call-done = bf16[2,16,10,128,128]{4,3,2,0,1:T(8,128)(2,1)} async-done(((bf16[2,1,10,128,128]{4,3,2,0,1:T(8,128)(2,1)}), bf16[2,16,10,128,128]{4,3,2,0,1:T(8,128)(2,1)}) %all-gather.6.cloned.1.call-update) | async-done | bytes 10485776 | tf_op jit(solution)/shard_map/all_gather | solution.py:66
  140.9 10.9 %fusion.3 = f32[16,4,128,128]{2,3,0,1:T(8,128)} fusion(bf16[2,16,10,128,128]{4,3,2,0,1:T(8,128)(2,1)} %all-gather.6.cloned.1.call-done, bf16[2,4,128,10,128,1]{4,3,2,1,0,5:T(8,128)(2,1)} %bitcast.172), kind=kOutput, calls=%fused_computation.5 | convolution fusion | flops 5368709120 | bytes 17301504 | tf_op jit(solution)/shard_map/caqux,cpuqy->apxy/dot_general | solution.py:68
  151.8 58.5 %all-reduce.2 = bf16[16,4,128,128]{2,3,0,1:T(8,128)(2,1)S(1)} all-reduce(f32[16,4,128,128]{2,3,0,1:T(8,128)} %fusion.3), channel_id=2, replica_groups=mesh['row'=8,'col'=16] {'row'}, use_global_device_ids=true, to_apply=%region_0.0.clone | all-reduce | flops 1048576 | bytes 6291456
  210.5 1.5 collective-permute-start
  212.1 3.5 %collective-permute-done = bf16[4,128,128]{2,1,0:T(8,128)(2,1)S(1)} collective-permute-done((bf16[4,128,128]{2,1,0:T(8,128)(2,1)S(1)}, bf16[4,128,128]{2,1,0:T(8,128)(2,1)S(1)}, u32[]{:S(2)}, u32[]{:S(2)}) %collective-permute-start) | collective-permute-done | bytes 131104 | tf_op jit(solution)/shard_map/ppermute | solution.py:11
  215.8 1.3 collective-permute-done.1
  217.2 3.0 %collective-permute-start.2 = (bf16[4,128,128]{2,1,0:T(8,128)(2,1)S(1)}, bf16[4,128,128]{2,1,0:T(8,128)(2,1)S(1)}, u32[]{:S(2)}, u32[]{:S(2)}) collective-permute-start(bf16[4,128,128]{2,1,0:T(8,128)(2,1)S(1)} %fusion.38), channel_id=1, source_target_pairs={{0,2},{1,3},{2,0},{3,1},{4,6},{5,7},{6,4},{7,5},{8,10},{9,11},{10,... | collective-permute-start | bytes 393224 | tf_op jit(solution)/shard_map/ppermute | solution.py:11
  220.2 4.1 %collective-permute-done.2 = bf16[4,128,128]{2,1,0:T(8,128)(2,1)S(1)} collective-permute-done((bf16[4,128,128]{2,1,0:T(8,128)(2,1)S(1)}, bf16[4,128,128]{2,1,0:T(8,128)(2,1)S(1)}, u32[]{:S(2)}, u32[]{:S(2)}) %collective-permute-start.2) | collective-permute-done | bytes 131104 | tf_op jit(solution)/shard_map/ppermute | solution.py:11
  224.6 1.3 collective-permute-done.3
  226.2 5.5 %collective-permute-done.4 = bf16[4,128,128]{2,1,0:T(8,128)(2,1)S(1)} collective-permute-done((bf16[4,128,128]{2,1,0:T(8,128)(2,1)S(1)}, bf16[4,128,128]{2,1,0:T(8,128)(2,1)S(1)}, u32[]{:S(2)}, u32[]{:S(2)}) %collective-permute-start.4) | collective-permute-done | bytes 131104 | tf_op jit(solution)/shard_map/ppermute | solution.py:11
  231.8 1.3 collective-permute-start.5
  233.2 3.7 %collective-permute-done.5 = bf16[4,128,128]{2,1,0:T(8,128)(2,1)S(1)} collective-permute-done((bf16[4,128,128]{2,1,0:T(8,128)(2,1)S(1)}, bf16[4,128,128]{2,1,0:T(8,128)(2,1)S(1)}, u32[]{:S(2)}, u32[]{:S(2)}) %collective-permute-start.5) | collective-permute-done | bytes 131104 | tf_op jit(solution)/shard_map/ppermute | solution.py:11
  237.5 5.7 %collective-permute-done.6 = bf16[4,128,128]{2,1,0:T(8,128)(2,1)S(1)} collective-permute-done((bf16[4,128,128]{2,1,0:T(8,128)(2,1)S(1)}, bf16[4,128,128]{2,1,0:T(8,128)(2,1)S(1)}, u32[]{:S(2)}, u32[]{:S(2)}) %collective-permute-start.6) | collective-permute-done | bytes 131104 | tf_op jit(solution)/shard_map/ppermute | solution.py:11
  243.4 6.4 %collective-permute-done.7 = bf16[4,128,128]{2,1,0:T(8,128)(2,1)S(1)} collective-permute-done((bf16[4,128,128]{2,1,0:T(8,128)(2,1)S(1)}, bf16[4,128,128]{2,1,0:T(8,128)(2,1)S(1)}, u32[]{:S(2)}, u32[]{:S(2)}) %collective-permute-start.7) | collective-permute-done | bytes 131104 | tf_op jit(solution)/shard_map/ppermute | solution.py:11
  250.0 2.9 %collective-permute-start.8 = (bf16[4,128,128]{2,1,0:T(8,128)(2,1)S(1)}, bf16[4,128,128]{2,1,0:T(8,128)(2,1)S(1)}, u32[]{:S(2)}, u32[]{:S(2)}) collective-permute-start(bf16[4,128,128]{2,1,0:T(8,128)(2,1)S(1)} %fusion.14), channel_id=1, source_target_pairs={{0,8},{1,9},{2,10},{3,11},{4,12},{5,13},{6,14},{7,15},{8,0},{9,1},... | collective-permute-start | bytes 393224 | tf_op jit(solution)/shard_map/ppermute | solution.py:11
  252.9 3.6 %collective-permute-done.8 = bf16[4,128,128]{2,1,0:T(8,128)(2,1)S(1)} collective-permute-done((bf16[4,128,128]{2,1,0:T(8,128)(2,1)S(1)}, bf16[4,128,128]{2,1,0:T(8,128)(2,1)S(1)}, u32[]{:S(2)}, u32[]{:S(2)}) %collective-permute-start.8) | collective-permute-done | bytes 131104 | tf_op jit(solution)/shard_map/ppermute | solution.py:11
  256.8 6.5 %collective-permute-done.9 = bf16[4,128,128]{2,1,0:T(8,128)(2,1)S(1)} collective-permute-done((bf16[4,128,128]{2,1,0:T(8,128)(2,1)S(1)}, bf16[4,128,128]{2,1,0:T(8,128)(2,1)S(1)}, u32[]{:S(2)}, u32[]{:S(2)}) %collective-permute-start.9) | collective-permute-done | bytes 131104 | tf_op jit(solution)/shard_map/ppermute | solution.py:11
  (45 shorter events, 5.5 us)
Async XLA Ops:
  6.5 102.2 %all-gather.4.cloned.1.call-start = ((), (), s32[]{:S(2)}) async-start(), calls=%async_computation.1 | async-start | bytes 5898240 | tf_op jit(solution)/shard_map/all_gather | solution.py:50
  7.3 133.6 %all-gather.6.cloned.1.call-start = ((), (), s32[]{:S(2)}) async-start(), calls=%async_computation.2 | async-start | bytes 11141120 | tf_op jit(solution)/shard_map/all_gather | solution.py:66
  12.0 8.2 %copy-start = (s32[2,1]{0,1:T(1,128)S(1)}, s32[2,1]{0,1:T(1,128)}, u32[]{:S(2)}) copy-start(s32[2,1]{0,1:T(1,128)} %param.5) | copy-start | bytes 28
  12.0 91.0 %copy-start.1 = (u32[128]{0:T(128)S(1)}, u32[128]{0:T(128)}, u32[]{:S(2)}) copy-start(u32[128]{0:T(128)} %constant.71) | copy-start | bytes 1540
  12.0 92.2 %all-to-all-start = ((bf16[16,2,1,4,128,128]{5,4,3,1,2,0:T(8,128)(2,1)}), bf16[16,2,1,4,128,128]{5,4,3,1,2,0:T(8,128)(2,1)}, u32[]{:S(2)}, u32[]{:S(2)}) async-start(bf16[16,2,1,4,128,128]{5,4,3,1,2,0:T(8,128)(2,1)} %stack.109), calls=%async_computation | async-start | bytes 8388608 | tf_op jit(solution)/shard_map/all_to_all | solution.py:55
  210.5 5.0 %collective-permute-start = (bf16[4,128,128]{2,1,0:T(8,128)(2,1)S(1)}, bf16[4,128,128]{2,1,0:T(8,128)(2,1)S(1)}, u32[]{:S(2)}, u32[]{:S(2)}) collective-permute-start(bf16[4,128,128]{2,1,0:T(8,128)(2,1)S(1)} %dynamic-slice_bitcast_fusion), channel_id=1, source_target_pairs={{0,1},{1,0},{2,3},{3,2},{4,5},{5,4},{6,7},{7,6},{8,9},{9,8},{10,11... | collective-permute-start | bytes 393224 | tf_op jit(solution)/shard_map/ppermute | solution.py:11
  215.7 1.4 collective-permute-start.1
  217.2 7.1 %collective-permute-start.2 = (bf16[4,128,128]{2,1,0:T(8,128)(2,1)S(1)}, bf16[4,128,128]{2,1,0:T(8,128)(2,1)S(1)}, u32[]{:S(2)}, u32[]{:S(2)}) collective-permute-start(bf16[4,128,128]{2,1,0:T(8,128)(2,1)S(1)} %fusion.38), channel_id=1, source_target_pairs={{0,2},{1,3},{2,0},{3,1},{4,6},{5,7},{6,4},{7,5},{8,10},{9,11},{10,... | collective-permute-start | bytes 393224 | tf_op jit(solution)/shard_map/ppermute | solution.py:11
  224.5 1.4 collective-permute-start.3
  226.1 5.6 %collective-permute-start.4 = (bf16[4,128,128]{2,1,0:T(8,128)(2,1)S(1)}, bf16[4,128,128]{2,1,0:T(8,128)(2,1)S(1)}, u32[]{:S(2)}, u32[]{:S(2)}) collective-permute-start(bf16[4,128,128]{2,1,0:T(8,128)(2,1)S(1)} %fusion.30), channel_id=1, source_target_pairs={{0,32},{16,48},{32,0},{48,16},{64,96},{80,112},{96,64},{112,80},{1... | collective-permute-start | bytes 393224 | tf_op jit(solution)/shard_map/ppermute | solution.py:11
  231.8 5.0 %collective-permute-start.5 = (bf16[4,128,128]{2,1,0:T(8,128)(2,1)S(1)}, bf16[4,128,128]{2,1,0:T(8,128)(2,1)S(1)}, u32[]{:S(2)}, u32[]{:S(2)}) collective-permute-start(bf16[4,128,128]{2,1,0:T(8,128)(2,1)S(1)} %fusion.26), channel_id=1, source_target_pairs={{0,4},{1,5},{2,6},{3,7},{4,0},{5,1},{6,2},{7,3},{8,12},{9,13},{10,... | collective-permute-start | bytes 393224 | tf_op jit(solution)/shard_map/ppermute | solution.py:11
  237.0 6.1 %collective-permute-start.6 = (bf16[4,128,128]{2,1,0:T(8,128)(2,1)S(1)}, bf16[4,128,128]{2,1,0:T(8,128)(2,1)S(1)}, u32[]{:S(2)}, u32[]{:S(2)}) collective-permute-start(bf16[4,128,128]{2,1,0:T(8,128)(2,1)S(1)} %fusion.22), channel_id=1, source_target_pairs={{0,32},{16,48},{32,0},{48,16},{64,96},{80,112},{96,64},{112,80},{1... | collective-permute-start | bytes 393224 | tf_op jit(solution)/shard_map/ppermute | solution.py:11
  243.3 6.6 %collective-permute-start.7 = (bf16[4,128,128]{2,1,0:T(8,128)(2,1)S(1)}, bf16[4,128,128]{2,1,0:T(8,128)(2,1)S(1)}, u32[]{:S(2)}, u32[]{:S(2)}) collective-permute-start(bf16[4,128,128]{2,1,0:T(8,128)(2,1)S(1)} %fusion.18), channel_id=1, source_target_pairs={{0,64},{16,80},{32,96},{48,112},{64,0},{80,16},{96,32},{112,48},{1... | collective-permute-start | bytes 393224 | tf_op jit(solution)/shard_map/ppermute | solution.py:11
  250.0 6.6 %collective-permute-start.8 = (bf16[4,128,128]{2,1,0:T(8,128)(2,1)S(1)}, bf16[4,128,128]{2,1,0:T(8,128)(2,1)S(1)}, u32[]{:S(2)}, u32[]{:S(2)}) collective-permute-start(bf16[4,128,128]{2,1,0:T(8,128)(2,1)S(1)} %fusion.14), channel_id=1, source_target_pairs={{0,8},{1,9},{2,10},{3,11},{4,12},{5,13},{6,14},{7,15},{8,0},{9,1},... | collective-permute-start | bytes 393224 | tf_op jit(solution)/shard_map/ppermute | solution.py:11
  256.7 6.6 %collective-permute-start.9 = (bf16[4,128,128]{2,1,0:T(8,128)(2,1)S(1)}, bf16[4,128,128]{2,1,0:T(8,128)(2,1)S(1)}, u32[]{:S(2)}, u32[]{:S(2)}) collective-permute-start(bf16[4,128,128]{2,1,0:T(8,128)(2,1)S(1)} %fusion.10), channel_id=1, source_target_pairs={{0,64},{16,80},{32,96},{48,112},{64,0},{80,16},{96,32},{112,48},{1... | collective-permute-start | bytes 393224 | tf_op jit(solution)/shard_map/ppermute | solution.py:11
Sparse Core Ops, SparseCore 0:
  9.0 38.9 all-gather.3
  50.2 90.6 all-gather.5
